TPU v7x, 512 devices: a whole 4x8x8 slice. The times are simulated.
512 devices in a mesh: dom: 64 (over y, z_hi, x), depth: 8 (over z_lo, core).
Axes of the slice: x: 4, y: 8, z: 8 (z_hi: 2, z_lo: 4; z = z_hi * 4 + z_lo), core: 2. Of those that a mesh axis runs over, the one named last changes fastest.
Arguments:
- ancestors: int32 [64], P('dom'), may hold values from 0 to 63, as said below
- ensemble: float32 [64, 4, 48, 16, 128], P('dom', None, 'depth'), may hold values from -4 to 4
- diffusivity: float32 [48, 16, 128], P('depth'), may hold values from 0.02 to 0.1
- melting_speed: float32 [48, 16, 128], P('depth'), may hold values from 0.05 to 0.3
- permeability: float32 [48, 16, 128], P('depth'), may hold values from 0.5 to 2
Outputs:
- forecast_ensemble: float32 [64, 4, 48, 16, 128], P('dom', None, 'depth')
Inputs may be any that keep to these rules, and one draw needn't show every extreme that they name: `ancestors`: each entry names a particle; slots 0 and 2 descend from particle 1, slot 1 from particle 0, slot 3 from particle 64 - 1.
All inputs are finite; a program needn't handle non-finite values.
Results may differ from a plain program's by a relative error of at most 0.00002.
Values sent between devices are 32-bit elements; how exact they have to be, the bound alone decides.
A program may use at most 64 MiB of HBM per device.

v0:
```python
import jax
import jax.numpy as jnp
from jax import lax
from jax.sharding import PartitionSpec as P

STEPS = 4


advect_coef = 0.1


def extended(block, sides, width):
    for axis, dim in sides:
        count = lax.axis_size(axis)
        forward = [(i, i + 1) for i in range(count - 1)]
        backward = [(target, source) for source, target in forward]
        low = lax.ppermute(
            lax.slice_in_dim(block, block.shape[dim] - width, None, axis=dim), axis, forward
        )
        high = lax.ppermute(lax.slice_in_dim(block, 0, width, axis=dim), axis, backward)
        block = jnp.concatenate([low, block, high], axis=dim)
    return block


def advance(padded, diffuse, reacts, permeab):
    center = padded[:, :, 1:-1]
    upper_cells = padded[:, :, :-2]
    lower_cells = padded[:, :, 2:]
    flat_pad = jnp.pad(center, ((0, 0), (0, 0), (0, 0), (1, 1), (1, 1)))
    laplacian_operator = (
        upper_cells + lower_cells + flat_pad[:, :, :, 2:, 1:-1] + flat_pad[:, :, :, :-2, 1:-1]
    )
    laplacian_operator = (
        laplacian_operator
        + flat_pad[:, :, :, 1:-1, 2:]
        + flat_pad[:, :, :, 1:-1, :-2]
        - 6.0 * center
    )
    velocity = center[:, 1]
    transport_update = advect_coef * jnp.maximum(velocity, 0.0)[:, None] * (center - upper_cells)
    transport_update = transport_update + advect_coef * jnp.minimum(velocity, 0.0)[:, None] * (
        lower_cells - center
    )
    fraction = center[:, 0]
    enthalpy = center[:, 2]
    composition = center[:, 3]
    melting = reacts * (enthalpy - 0.5 * composition)
    new_fraction = fraction - transport_update[:, 0] + melting
    new_velocity = (
        velocity + 0.2 * (permeab * jnp.tanh(fraction) - velocity) + 0.1 * laplacian_operator[:, 1]
    )
    new_enthalpy = (
        enthalpy - transport_update[:, 2] + diffuse * laplacian_operator[:, 2] - 0.5 * melting
    )
    new_composition = composition - transport_update[:, 3] + diffuse * laplacian_operator[:, 3]
    return jnp.stack([new_fraction, new_velocity, new_enthalpy, new_composition], axis=1)


def predict_forward(field_stack, diffusivity, melting_speed, permeability):

    def one_step(step_index, present_members):
        padded = extended(present_members, (("depth", 2),), 1)
        return advance(padded, diffusivity, melting_speed, permeability)

    return lax.fori_loop(0, STEPS, one_step, field_stack)


def local(ancestors, ensemble, diffusivity, melting_speed, permeability):
    source = ancestors[0]
    shard_rows = lax.all_gather(ensemble, "dom", axis=0, tiled=True)
    indices = jnp.arange(shard_rows.shape[0], dtype=jnp.int32)
    chosen = (indices == source).reshape((-1, 1, 1, 1, 1))
    present_members = jnp.sum(jnp.where(chosen, shard_rows, 0.0), axis=0, keepdims=True)
    return predict_forward(present_members, diffusivity, melting_speed, permeability)


def solution(mesh):
    return jax.shard_map(
        local,
        mesh=mesh,
        in_specs=(
            P("dom"),
            P("dom", None, "depth", None, None),
            P("depth", None, None),
            P("depth", None, None),
            P("depth", None, None),
        ),
        out_specs=P("dom", None, "depth", None, None),
        check_vma=False,
    )
```

profile of v0, /device:TPU:1, one launch (start us, length us, event | category | flops | bytes accessed | tf_op | source)
XLA Modules:
  0.0 308.2 jit_solution(16970929939800095742)
XLA Ops:
  6.5 0.0 copy-start.1
  6.5 0.0 copy-start.2
  6.5 0.0 copy-start.3
  6.5 0.0 all-gather.2.cloned.1.call-start
  6.5 0.7 all-gather.2.cloned.1.call-update
  7.9 257.1 %all-gather.2.cloned.1.call-done = f32[64,4,6,16,128]{4,3,2,1,0:T(8,128)} async-done(((f32[1,4,6,16,128]{4,3,2,1,0:T(8,128)}), f32[64,4,6,16,128]{4,3,2,1,0:T(8,128)}) %all-gather.2.cloned.1.call-update) | async-done | bytes 12582928 | tf_op jit(solution)/shard_map/all_gather | solution.py:70
  265.0 6.4 %select_reduce_fusion = f32[4,6,16,128]{3,2,1,0:T(8,128)S(1)} fusion(f32[64,4,6,16,128]{4,3,2,1,0:T(8,128)} %all-gather.2.cloned.1.call-done, pred[64]{0:T(512)(128)(4,1)S(1)} %iota_compare_fusion), kind=kLoop, calls=%fused_computation.36 | loop fusion | flops 6242304 | bytes 12779584 | tf_op jit(solution)/shard_map/reduce_sum | solution.py:73
  271.4 0.0 copy-done.1
  271.4 0.0 copy-done.2
  271.4 0.0 copy-done.3
  271.5 29.2 %while.12 = (s32[]{:T(128)}, f32[1,4,6,16,128]{4,3,2,1,0:T(8,128)S(1)}, f32[6,16,128]{2,1,0:T(8,128)S(1)}, f32[6,16,128]{2,1,0:T(8,128)S(1)}, f32[6,16,128]{2,1,0:T(8,128)S(1)}, /*index=5*/s32[]{:T(128)}) while((s32[]{:T(128)}, f32[1,4,6,16,128]{4,3,2,1,0:T(8,128)S(1)}, f32[6,16,128]{2,1,0:T(8,128)S(1)}, f32[6,16,128]{2,1,0:T(8,128)S(1)}, ...), condition=%wide.region_2.3_spmd, body=%wide.region_1.2_spmd.sunk | while | flops 1118210 | bytes 2523285 | solution.py:65
  271.5 3.0 collective-permute-start
  274.5 2.6 collective-permute-start.1
  277.1 0.0 collective-permute-done
  277.1 1.0 collective-permute-done.1
  278.1 0.2 fusion.24
  278.2 0.1 fusion.25
  278.3 1.9 collective-permute-start
  280.3 4.2 %collective-permute-start.1 = (f32[1,4,1,16,128]{4,3,2,1,0:T(8,128)S(1)}, f32[1,4,1,16,128]{4,3,2,1,0:T(8,128)S(1)}, u32[]{:S(2)}, u32[]{:S(2)}) collective-permute-start(f32[1,4,1,16,128]{4,3,2,1,0:T(8,128)S(1)} %get-tuple-element.133), channel_id=1, source_target_pairs={{0,1},{1,2},{2,3},{3,4},{4,5},{5,6},{6,7},{8,9},{9,10},{10,11},{11... | collective-permute-start | bytes 98312 | tf_op jit(solution)/shard_map/while/body/eval_jaxpr/ppermute | solution.py:17
  284.5 0.0 collective-permute-done
  284.5 1.0 collective-permute-done.1
  285.5 0.2 fusion.24
  285.7 0.1 fusion.25
  285.8 1.9 collective-permute-start
  287.7 4.2 %collective-permute-start.1 = (f32[1,4,1,16,128]{4,3,2,1,0:T(8,128)S(1)}, f32[1,4,1,16,128]{4,3,2,1,0:T(8,128)S(1)}, u32[]{:S(2)}, u32[]{:S(2)}) collective-permute-start(f32[1,4,1,16,128]{4,3,2,1,0:T(8,128)S(1)} %get-tuple-element.133), channel_id=1, source_target_pairs={{0,1},{1,2},{2,3},{3,4},{4,5},{5,6},{6,7},{8,9},{9,10},{10,11},{11... | collective-permute-start | bytes 98312 | tf_op jit(solution)/shard_map/while/body/eval_jaxpr/ppermute | solution.py:17
  292.0 0.0 collective-permute-done
  292.0 1.0 collective-permute-done.1
  293.0 0.2 fusion.24
  293.1 0.1 fusion.25
  293.2 1.9 collective-permute-start
  295.2 4.2 %collective-permute-start.1 = (f32[1,4,1,16,128]{4,3,2,1,0:T(8,128)S(1)}, f32[1,4,1,16,128]{4,3,2,1,0:T(8,128)S(1)}, u32[]{:S(2)}, u32[]{:S(2)}) collective-permute-start(f32[1,4,1,16,128]{4,3,2,1,0:T(8,128)S(1)} %get-tuple-element.133), channel_id=1, source_target_pairs={{0,1},{1,2},{2,3},{3,4},{4,5},{5,6},{6,7},{8,9},{9,10},{10,11},{11... | collective-permute-start | bytes 98312 | tf_op jit(solution)/shard_map/while/body/eval_jaxpr/ppermute | solution.py:17
  299.4 0.0 collective-permute-done
  299.4 1.0 collective-permute-done.1
  300.4 0.2 fusion.24
  300.6 0.1 fusion.25
  300.7 0.0 copy-start
  300.7 0.7 copy-done
  (13 shorter events, 0.1 us)
Async XLA Ops:
  6.5 264.9 %copy-start.1 = (f32[6,16,128]{2,1,0:T(8,128)S(1)}, f32[6,16,128]{2,1,0:T(8,128)}, u32[]{:S(2)}) copy-start(f32[6,16,128]{2,1,0:T(8,128)} %param.10) | copy-start | bytes 147460
  6.5 264.9 %copy-start.2 = (f32[6,16,128]{2,1,0:T(8,128)S(1)}, f32[6,16,128]{2,1,0:T(8,128)}, u32[]{:S(2)}) copy-start(f32[6,16,128]{2,1,0:T(8,128)} %param.11) | copy-start | bytes 147460
  6.5 264.9 %copy-start.3 = (f32[6,16,128]{2,1,0:T(8,128)S(1)}, f32[6,16,128]{2,1,0:T(8,128)}, u32[]{:S(2)}) copy-start(f32[6,16,128]{2,1,0:T(8,128)} %param.9) | copy-start | bytes 147460
  6.5 258.5 %all-gather.2.cloned.1.call-start = ((), (), s32[]{:S(2)}) async-start(), calls=%async_computation | async-start | bytes 12779520 | tf_op jit(solution)/shard_map/all_gather | solution.py:70
  271.5 5.6 %collective-permute-start = (f32[1,4,1,16,128]{4,3,2,1,0:T(8,128)S(1)}, f32[1,4,1,16,128]{4,3,2,1,0:T(8,128)S(1)}, u32[]{:S(2)}, u32[]{:S(2)}) collective-permute-start(f32[1,4,1,16,128]{4,3,2,1,0:T(8,128)S(1)} %get-tuple-element.132), channel_id=1, source_target_pairs={{1,0},{2,1},{3,2},{4,3},{5,4},{6,5},{7,6},{9,8},{10,9},{11,10},{12... | collective-permute-start | bytes 98312 | tf_op jit(solution)/shard_map/while/body/eval_jaxpr/ppermute | solution.py:20
  274.5 3.6 %collective-permute-start.1 = (f32[1,4,1,16,128]{4,3,2,1,0:T(8,128)S(1)}, f32[1,4,1,16,128]{4,3,2,1,0:T(8,128)S(1)}, u32[]{:S(2)}, u32[]{:S(2)}) collective-permute-start(f32[1,4,1,16,128]{4,3,2,1,0:T(8,128)S(1)} %get-tuple-element.133), channel_id=1, source_target_pairs={{0,1},{1,2},{2,3},{3,4},{4,5},{5,6},{6,7},{8,9},{9,10},{10,11},{11... | collective-permute-start | bytes 98312 | tf_op jit(solution)/shard_map/while/body/eval_jaxpr/ppermute | solution.py:17
  278.3 6.2 %collective-permute-start = (f32[1,4,1,16,128]{4,3,2,1,0:T(8,128)S(1)}, f32[1,4,1,16,128]{4,3,2,1,0:T(8,128)S(1)}, u32[]{:S(2)}, u32[]{:S(2)}) collective-permute-start(f32[1,4,1,16,128]{4,3,2,1,0:T(8,128)S(1)} %get-tuple-element.132), channel_id=1, source_target_pairs={{1,0},{2,1},{3,2},{4,3},{5,4},{6,5},{7,6},{9,8},{10,9},{11,10},{12... | collective-permute-start | bytes 98312 | tf_op jit(solution)/shard_map/while/body/eval_jaxpr/ppermute | solution.py:20
  280.3 5.2 %collective-permute-start.1 = (f32[1,4,1,16,128]{4,3,2,1,0:T(8,128)S(1)}, f32[1,4,1,16,128]{4,3,2,1,0:T(8,128)S(1)}, u32[]{:S(2)}, u32[]{:S(2)}) collective-permute-start(f32[1,4,1,16,128]{4,3,2,1,0:T(8,128)S(1)} %get-tuple-element.133), channel_id=1, source_target_pairs={{0,1},{1,2},{2,3},{3,4},{4,5},{5,6},{6,7},{8,9},{9,10},{10,11},{11... | collective-permute-start | bytes 98312 | tf_op jit(solution)/shard_map/while/body/eval_jaxpr/ppermute | solution.py:17
  285.8 6.2 %collective-permute-start = (f32[1,4,1,16,128]{4,3,2,1,0:T(8,128)S(1)}, f32[1,4,1,16,128]{4,3,2,1,0:T(8,128)S(1)}, u32[]{:S(2)}, u32[]{:S(2)}) collective-permute-start(f32[1,4,1,16,128]{4,3,2,1,0:T(8,128)S(1)} %get-tuple-element.132), channel_id=1, source_target_pairs={{1,0},{2,1},{3,2},{4,3},{5,4},{6,5},{7,6},{9,8},{10,9},{11,10},{12... | collective-permute-start | bytes 98312 | tf_op jit(solution)/shard_map/while/body/eval_jaxpr/ppermute | solution.py:20
  287.7 5.2 %collective-permute-start.1 = (f32[1,4,1,16,128]{4,3,2,1,0:T(8,128)S(1)}, f32[1,4,1,16,128]{4,3,2,1,0:T(8,128)S(1)}, u32[]{:S(2)}, u32[]{:S(2)}) collective-permute-start(f32[1,4,1,16,128]{4,3,2,1,0:T(8,128)S(1)} %get-tuple-element.133), channel_id=1, source_target_pairs={{0,1},{1,2},{2,3},{3,4},{4,5},{5,6},{6,7},{8,9},{9,10},{10,11},{11... | collective-permute-start | bytes 98312 | tf_op jit(solution)/shard_map/while/body/eval_jaxpr/ppermute | solution.py:17
  293.2 6.2 %collective-permute-start = (f32[1,4,1,16,128]{4,3,2,1,0:T(8,128)S(1)}, f32[1,4,1,16,128]{4,3,2,1,0:T(8,128)S(1)}, u32[]{:S(2)}, u32[]{:S(2)}) collective-permute-start(f32[1,4,1,16,128]{4,3,2,1,0:T(8,128)S(1)} %get-tuple-element.132), channel_id=1, source_target_pairs={{1,0},{2,1},{3,2},{4,3},{5,4},{6,5},{7,6},{9,8},{10,9},{11,10},{12... | collective-permute-start | bytes 98312 | tf_op jit(solution)/shard_map/while/body/eval_jaxpr/ppermute | solution.py:20
  295.2 5.2 %collective-permute-start.1 = (f32[1,4,1,16,128]{4,3,2,1,0:T(8,128)S(1)}, f32[1,4,1,16,128]{4,3,2,1,0:T(8,128)S(1)}, u32[]{:S(2)}, u32[]{:S(2)}) collective-permute-start(f32[1,4,1,16,128]{4,3,2,1,0:T(8,128)S(1)} %get-tuple-element.133), channel_id=1, source_target_pairs={{0,1},{1,2},{2,3},{3,4},{4,5},{5,6},{6,7},{8,9},{9,10},{10,11},{11... | collective-permute-start | bytes 98312 | tf_op jit(solution)/shard_map/while/body/eval_jaxpr/ppermute | solution.py:17
  300.7 0.7 copy-start
Sparse Core Ops, SparseCore 0:
  11.8 253.2 all-gather.1
where the time goes:
time: 309 us; the launch traced here: 308 us
  waiting for transfers between devices  262 us (85%)
  starting transfers between devices  24 us (8%)
  between operations  14.1 us (5%)
  other arithmetic  7.4 us (2%)
    all_gather x1, waiting for transfers between devices, local(): shard_rows = lax.all_gather(ensemble, 'dom', axis=0, tiled=True)  257 us
    ppermute x4, starting transfers between devices, extended(): lax.ppermute(lax.slice_in_dim(block, block.shape[dim] - width, None, axis...  15.2 us
    ppermute x4, starting transfers between devices, extended(): lax.ppermute(lax.slice_in_dim(block, 0, width, axis=dim), axis, backward)  8.77 us
    reduce_sum x1, other arithmetic, local(): jnp.sum(jnp.where(chosen, shard_rows, 0.0), axis=0, keepdims=True)  6.39 us
  transfers between devices with their start and end apart: 9, of which 5 were waited for; matrix products, arithmetic and copies ran while one was open for 0% of the time, Pallas kernels for 0%

commit v1 on v0

v1 whole, which is shorter than its diff:
```python
import functools

import jax
import jax.numpy as jnp
from jax import lax
from jax.experimental import pallas as pl
from jax.experimental.pallas import tpu as pltpu
from jax.sharding import PartitionSpec as P

STEPS = 4
FIELDS = 4
DOM = 64
DEPTH = 8
LAYERS = 6
NX = 16
NY = 128
TILE = 8
TILES = FIELDS * LAYERS * NX // TILE
HALO = STEPS
EXT = LAYERS + 2 * HALO
COEF_HALO = STEPS - 1

advect_coef = 0.1


def remote(src, dst, send_sem, recv_sem, **where):
    return pltpu.make_async_remote_copy(
        src_ref=src,
        dst_ref=dst,
        send_sem=send_sem,
        recv_sem=recv_sem,
        device_id=where,
        device_id_type=pl.DeviceIdType.MESH,
    )


def holder_of(row, i, dp):
    return row * 4 + lax.rem(row + dp + 1 + i, 4)


def resample_kernel(
    anc_ref,
    ens_ref,
    dif_ref,
    spd_ref,
    per_ref,
    state_ref,
    coef_ref,
    held,
    out_tiles,
    anc_send,
    anc_recv,
    anc_row,
    anc_smem,
    anc_sems,
    smem_sem,
    p1_send,
    p1_recv,
    p2_send,
    p2_recv,
    halo_send,
    halo_recv,
    coef_send,
    coef_recv,
):
    me = lax.axis_index("dom")
    dp = lax.axis_index("depth")
    my_row = me // 4
    my_i = lax.rem(lax.rem(me, 4) - my_row - dp - 1 + 64, 4)
    is_holder = my_i != 3
    my_tile = my_row * 3 + my_i
    has_low = dp > 0
    has_high = dp < DEPTH - 1

    barrier = pltpu.get_barrier_semaphore()

    def greet(t, carry):
        pl.semaphore_signal(
            barrier,
            inc=1,
            device_id={"dom": me ^ t},
            device_id_type=pl.DeviceIdType.MESH,
        )
        return carry

    @pl.when(has_low)
    def _():
        pl.semaphore_signal(
            barrier, inc=1, device_id={"depth": dp - 1}, device_id_type=pl.DeviceIdType.MESH
        )

    @pl.when(has_high)
    def _():
        pl.semaphore_signal(
            barrier, inc=1, device_id={"depth": dp + 1}, device_id_type=pl.DeviceIdType.MESH
        )

    lax.fori_loop(1, DOM, greet, 0)
    lane = lax.broadcasted_iota(jnp.int32, (1, 128), 1)
    anc_send[0] = jnp.where(lane == me, anc_ref[0], 0)
    pl.semaphore_wait(
        barrier, DOM - 1 + has_low.astype(jnp.int32) + has_high.astype(jnp.int32)
    )

    def anc_hop(hop, stride):
        def start(t, carry):
            remote(
                anc_send.at[hop],
                anc_recv.at[hop, t],
                anc_sems.at[2 * hop],
                anc_sems.at[2 * hop + 1],
                dom=me ^ (t * stride),
            ).start()
            return carry

        lax.fori_loop(1, 8, start, 0)

    def anc_done(hop):
        view = anc_recv.at[hop, pl.ds(1, 7)]
        pltpu.make_async_copy(view, view, anc_sems.at[2 * hop + 1]).wait()
        total = anc_send[hop]
        for t in range(1, 8):
            total = total + anc_recv[hop, t]
        return total

    anc_hop(0, 8)

    def spread(n, carry):
        row = (n // 3) ^ my_row
        i = lax.rem(n, 3)
        target = holder_of(row, i, dp)
        p = row * 3 + i

        @pl.when(target != me)
        def _():
            remote(ens_ref.at[p], held.at[me], p1_send, p1_recv, dom=target).start()

        @pl.when(target == me)
        def _():
            pltpu.make_async_copy(ens_ref.at[p], held.at[me], p1_send).start()

        return carry

    lax.fori_loop(0, TILES, spread, 0)

    coefs = (dif_ref, spd_ref, per_ref)

    def coef_to_low(c):
        return remote(
            coefs[c].at[pl.ds(0, COEF_HALO)],
            coef_ref.at[1, c],
            coef_send.at[0, c],
            coef_recv.at[1, c],
            depth=dp - 1,
        )

    def coef_to_high(c):
        return remote(
            coefs[c].at[pl.ds(LAYERS - COEF_HALO, COEF_HALO)],
            coef_ref.at[0, c],
            coef_send.at[1, c],
            coef_recv.at[0, c],
            depth=dp + 1,
        )

    anc_send[1] = anc_done(0)
    anc_hop(1, 1)

    @pl.when(has_low)
    def _():
        for c in range(3):
            coef_to_low(c).start()

    @pl.when(has_high)
    def _():
        for c in range(3):
            coef_to_high(c).start()

    anc_row[...] = anc_done(1)
    to_smem = pltpu.make_async_copy(anc_row, anc_smem, smem_sem)
    to_smem.start()
    to_smem.wait()

    state_tiles = state_ref

    f = my_tile // 12
    rest = lax.rem(my_tile, 12)
    layer = rest // 2 + HALO
    half = lax.rem(rest, 2)

    pltpu.make_async_copy(held.at[pl.ds(0, TILES)], held.at[pl.ds(0, TILES)], p1_send).wait()

    @pl.when(is_holder)
    def _():
        pltpu.make_async_copy(
            held.at[pl.ds(0, DOM - 1)], held.at[pl.ds(0, DOM - 1)], p1_recv
        ).wait()
        place = state_tiles.at[f, layer, half]

        def give(t, carry):
            target = me ^ t
            out_tiles[t] = held[anc_smem[0, target]]
            remote(out_tiles.at[t], place, p2_send, p2_recv, dom=target).start()
            return carry

        lax.fori_loop(1, DOM, give, 0)
        out_tiles[0] = held[anc_smem[0, me]]
        pltpu.make_async_copy(out_tiles.at[0], place, p2_recv).start()

    own = held.at[pl.ds(0, TILES)]
    pltpu.make_async_copy(own, own, p2_recv).wait()

    to_low = remote(
        state_ref.at[:, pl.ds(HALO, HALO)],
        state_ref.at[:, pl.ds(HALO + LAYERS, HALO)],
        halo_send.at[0],
        halo_recv.at[1],
        depth=dp - 1,
    )
    to_high = remote(
        state_ref.at[:, pl.ds(LAYERS, HALO)],
        state_ref.at[:, pl.ds(0, HALO)],
        halo_send.at[1],
        halo_recv.at[0],
        depth=dp + 1,
    )

    @pl.when(has_low)
    def _():
        to_low.start()

    @pl.when(has_high)
    def _():
        to_high.start()

    @pl.when(is_holder)
    def _():
        sent = out_tiles.at[pl.ds(1, DOM - 1)]
        pltpu.make_async_copy(sent, sent, p2_send).wait()

    for hop in range(2):
        view = anc_recv.at[hop, pl.ds(1, 7)]
        pltpu.make_async_copy(view, view, anc_sems.at[2 * hop]).wait()

    @pl.when(has_low)
    def _():
        for c in range(3):
            coef_to_low(c).wait_send()
            coef_to_high(c).wait_recv()
        to_low.wait_send()
        to_high.wait_recv()

    @pl.when(has_high)
    def _():
        for c in range(3):
            coef_to_high(c).wait_send()
            coef_to_low(c).wait_recv()
        to_high.wait_send()
        to_low.wait_recv()


def forecast_kernel(state_ref, halo_ref, dif_ref, spd_ref, per_ref, out_ref, a_ref, b_ref):
    dp = lax.axis_index("depth")
    has_low = dp > 0
    has_high = dp < DEPTH - 1
    row = lax.broadcasted_iota(jnp.int32, (NX, NY), 0)
    col = lax.broadcasted_iota(jnp.int32, (NX, NY), 1)
    first_row, last_row = row == 0, row == NX - 1
    first_col, last_col = col == 0, col == NY - 1
    inner = (dif_ref, spd_ref, per_ref)

    def coef(c, e):
        if e < HALO:
            return halo_ref[0, c, e - (HALO - COEF_HALO)]
        if e >= HALO + LAYERS:
            return halo_ref[1, c, e - HALO - LAYERS]
        return inner[c][e - HALO]

    def inside(e, x):
        if e < HALO:
            return jnp.where(has_low, x, 0.0)
        if e >= HALO + LAYERS:
            return jnp.where(has_high, x, 0.0)
        return x

    def flat(x):
        down = jnp.where(first_row, 0.0, pltpu.roll(x, 1, 0))
        up = jnp.where(last_row, 0.0, pltpu.roll(x, NX - 1, 0))
        right = jnp.where(first_col, 0.0, pltpu.roll(x, 1, 1))
        left = jnp.where(last_col, 0.0, pltpu.roll(x, NY - 1, 1))
        return (down + up) + (right + left)

    for step in range(STEPS):
        src = (None, a_ref, b_ref, a_ref)[step]
        dst = (a_ref, b_ref, a_ref, None)[step]

        def load(f, e):
            if src is None:
                return inside(e, state_ref[f, e])
            return src[f, e]

        for e in range(step + 1, EXT - 1 - step):
            m, v, h, c = (load(f, e) for f in range(FIELDS))
            mu, vu, hu, cu = (load(f, e - 1) for f in range(FIELDS))
            ml, vl, hl, cl = (load(f, e + 1) for f in range(FIELDS))
            diffuse, reacts, permeab = coef(0, e), coef(1, e), coef(2, e)
            vp = advect_coef * jnp.maximum(v, 0.0)
            vn = advect_coef * jnp.minimum(v, 0.0)

            def transport(q, qu, ql):
                return vp * (q - qu) + vn * (ql - q)

            def laplace(q, qu, ql):
                return qu + ql + flat(q) - 6.0 * q

            melting = reacts * (h - 0.5 * c)
            new = (
                m - transport(m, mu, ml) + melting,
                v + 0.2 * (permeab * jnp.tanh(m) - v) + 0.1 * laplace(v, vu, vl),
                h - transport(h, hu, hl) + diffuse * laplace(h, hu, hl) - 0.5 * melting,
                c - transport(c, cu, cl) + diffuse * laplace(c, cu, cl),
            )
            for f in range(FIELDS):
                if dst is None:
                    out_ref[f, e - HALO] = new[f]
                else:
                    dst[f, e] = inside(e, new[f])


def local(ancestors, ensemble, diffusivity, melting_speed, permeability):
    any_spec = pl.BlockSpec(memory_space=pl.ANY)
    tiles = ensemble.reshape(TILES, TILE, NY)
    split = (LAYERS, NX // TILE, TILE, NY)
    coefs = [c.reshape(split) for c in (diffusivity, melting_speed, permeability)]
    dma = pltpu.SemaphoreType.DMA
    state, halo = pl.pallas_call(
        resample_kernel,
        out_shape=(
            jax.ShapeDtypeStruct((FIELDS, EXT, NX // TILE, TILE, NY), jnp.float32),
            jax.ShapeDtypeStruct((2, 3, COEF_HALO, NX // TILE, TILE, NY), jnp.float32),
        ),
        in_specs=[pl.BlockSpec(memory_space=pltpu.SMEM)] + [any_spec] * 4,
        out_specs=(any_spec, any_spec),
        scratch_shapes=[
            pltpu.VMEM((DOM, TILE, NY), jnp.float32),
            pltpu.VMEM((DOM, TILE, NY), jnp.float32),
            pltpu.VMEM((2, 1, 128), jnp.int32),
            pltpu.VMEM((2, 8, 1, 128), jnp.int32),
            pltpu.VMEM((1, 128), jnp.int32),
            pltpu.SMEM((1, 128), jnp.int32),
            dma((4,)),
            dma,
            dma,
            dma,
            dma,
            dma,
            dma((2,)),
            dma((2,)),
            dma((2, 3)),
            dma((2, 3)),
        ],
        compiler_params=pltpu.CompilerParams(collective_id=0, has_side_effects=True),
    )(ancestors, tiles, *coefs)
    state = state.reshape(FIELDS, EXT, NX, NY)
    halo = halo.reshape(2, 3, COEF_HALO, NX, NY)
    vmem = pl.BlockSpec(memory_space=pltpu.VMEM)
    out = pl.pallas_call(
        forecast_kernel,
        out_shape=jax.ShapeDtypeStruct((FIELDS, LAYERS, NX, NY), jnp.float32),
        in_specs=[vmem] * 5,
        out_specs=vmem,
        scratch_shapes=[pltpu.VMEM((FIELDS, EXT, NX, NY), jnp.float32)] * 2,
    )(state, halo, diffusivity, melting_speed, permeability)
    return out[None]


def solution(mesh):
    return jax.shard_map(
        local,
        mesh=mesh,
        in_specs=(
            P("dom"),
            P("dom", None, "depth", None, None),
            P("depth", None, None),
            P("depth", None, None),
            P("depth", None, None),
        ),
        out_specs=P("dom", None, "depth", None, None),
        check_vma=False,
    )
```

time: 309 us -> 49.2 us (0.16)
  waiting for transfers between devices: 262 us -> 0 us
  Pallas kernels: 0 us -> 48.4 us
  starting transfers between devices: 24 us -> 0 us
  between operations: 14.1 us -> 0.66 us
  other arithmetic: 7.4 us -> 0 us
    all_gather x1 -> x0, waiting for transfers between devices: 257 us -> none  [local(): shard_rows = lax.all_gather(ensemble, 'dom', axis=0, tiled=True)]
    pallas_call x0 -> x2, Pallas kernels: none -> 48.4 us  [the longest x1 45.8 us: local(): pl.pallas_call(resample_kernel, out_shape=(jax.ShapeDtypeStruct((FIELDS,...]
    ppermute x8 -> x0, starting transfers between devices: 24 us -> none  [the longest x4 15.2 us: extended(): lax.ppermute(lax.slice_in_dim(block, block.shape[dim] - width, None, axis...]
    reduce_sum x1 -> x0, other arithmetic: 6.39 us -> none  [local(): jnp.sum(jnp.where(chosen, shard_rows, 0.0), axis=0, keepdims=True)]
    ppermute x8 -> x0, waiting for transfers between devices: 3.89 us -> none  [the longest x4 3.88 us: extended(): lax.ppermute(lax.slice_in_dim(block, block.shape[dim] - width, None, axis...]
  transfers between devices with their start and end apart: 9 -> 0, of which waited for: 5 -> 0; matrix products, arithmetic and copies ran while one was open for 0% -> 0% of each run, Pallas kernels for 0% -> 0%
where the time goes in v1:
time: 49.2 us; the launch traced here: 49.1 us
  Pallas kernels  48.4 us (98%)
  between operations  0.66 us (1%)
    pallas_call x1, Pallas kernels, local(): pl.pallas_call(resample_kernel, out_shape=(jax.ShapeDtypeStruct((FIELDS,...  45.8 us
    pallas_call x1, Pallas kernels, local(): pl.pallas_call(forecast_kernel, out_shape=jax.ShapeDtypeStruct((FIELDS, L...  2.6 us

profile of v1, /device:TPU:1, one launch (start us, length us, event | category | flops | bytes accessed | tf_op | source)
XLA Modules:
  0.0 49.1 jit_solution(14797182871570915018)
XLA Ops:
  0.7 45.8 %shard_map.55 = (f32[4,14,2,8,128]{4,3,2,1,0:T(8,128)}, f32[2,3,3,2,8,128]{5,4,3,2,1,0:T(8,128)}) custom-call(s32[1]{0:T(128)S(6)} %copy.6.anc_ref, f32[48,8,128]{2,1,0:T(8,128)} %bitcast.8, f32[6,2,8,128]{3,2,1,0:T(8,128)} %bitcast.9, f32[6,2,8,128]{3,2,1,0:T(8,128)} %bitcast.10, f32[6,2,8,128]{3,2,1,0:T(8,128)} %bitcast.11), custom_call_target="tpu_custom_call" | custom-call | tf_op jit(solution)/shard_map/pallas_call | solution.py:336
  46.5 2.6 %shard_map.56 = f32[4,6,16,128]{3,2,1,0:T(8,128)} custom-call(f32[4,14,16,128]{3,2,1,0:T(8,128)} %bitcast.7, f32[2,3,3,16,128]{4,3,2,1,0:T(8,128)} %bitcast.12, f32[6,16,128]{2,1,0:T(8,128)} %dif_ref.1, f32[6,16,128]{2,1,0:T(8,128)} %spd_ref.1, f32[6,16,128]{2,1,0:T(8,128)} %per_ref.1), custom_call_target="tpu_custom_call" | custom-call | tf_op jit(solution)/shard_map/pallas_call | solution.py:367

commit v2 on v1

--- a/solution.py
+++ b/solution.py
@@ -1,5 +1,3 @@
-import functools
-
 import jax
 import jax.numpy as jnp
 from jax import lax
@@ -15,7 +13,7 @@
 NX = 16
 NY = 128
 TILE = 8
-TILES = FIELDS * LAYERS * NX // TILE
+HOLDERS = FIELDS * LAYERS * NX // TILE
 HALO = STEPS
 EXT = LAYERS + 2 * HALO
 COEF_HALO = STEPS - 1
@@ -34,8 +32,12 @@
     )
 
 
-def holder_of(row, i, dp):
-    return row * 4 + lax.rem(row + dp + 1 + i, 4)
+def split_dom(index):
+    return index // 8, lax.rem(index // 4, 2), lax.rem(index, 4)
+
+
+def join_dom(y, z_hi, x):
+    return y * 8 + z_hi * 4 + x
 
 
 def resample_kernel(
@@ -47,15 +49,16 @@
     state_ref,
     coef_ref,
     held,
-    out_tiles,
+    chosen,
     anc_send,
     anc_recv,
     anc_row,
-    anc_smem,
+    anc_all,
     anc_sems,
     smem_sem,
     p1_send,
     p1_recv,
+    local_sem,
     p2_send,
     p2_recv,
     halo_send,
@@ -65,10 +68,9 @@
 ):
     me = lax.axis_index("dom")
     dp = lax.axis_index("depth")
-    my_row = me // 4
-    my_i = lax.rem(lax.rem(me, 4) - my_row - dp - 1 + 64, 4)
-    is_holder = my_i != 3
-    my_tile = my_row * 3 + my_i
+    my_y, my_z, my_x = split_dom(me)
+    my_tile = jnp.where(my_z == 0, my_y, DOM // 8 + lax.rem(my_y + 1, 8)) * 4 + my_x
+    is_holder = my_tile < HOLDERS
     has_low = dp > 0
     has_high = dp < DEPTH - 1
 
@@ -83,6 +85,16 @@
         )
         return carry
 
+    @pl.when(is_holder)
+    def _():
+        lax.fori_loop(1, DOM, greet, 0)
+
+    @pl.when(jnp.logical_not(is_holder))
+    def _():
+        for t in range(1, 8):
+            greet(t, 0)
+            greet(8 * t, 0)
+
     @pl.when(has_low)
     def _():
         pl.semaphore_signal(
@@ -95,15 +107,23 @@
             barrier, inc=1, device_id={"depth": dp + 1}, device_id_type=pl.DeviceIdType.MESH
         )
 
-    lax.fori_loop(1, DOM, greet, 0)
     lane = lax.broadcasted_iota(jnp.int32, (1, 128), 1)
     anc_send[0] = jnp.where(lane == me, anc_ref[0], 0)
+    other = jnp.where(is_holder, 0, 1)
+    far_row = jnp.where((my_y >= 3) & (my_y <= 6), 1, 0)
     pl.semaphore_wait(
-        barrier, DOM - 1 + has_low.astype(jnp.int32) + has_high.astype(jnp.int32)
+        barrier,
+        HOLDERS
+        - is_holder.astype(jnp.int32)
+        + 4 * my_z
+        + 4 * far_row
+        - 2 * other
+        + has_low.astype(jnp.int32)
+        + has_high.astype(jnp.int32),
     )
 
     def anc_hop(hop, stride):
-        def start(t, carry):
+        for t in range(1, 8):
             remote(
                 anc_send.at[hop],
                 anc_recv.at[hop, t],
@@ -111,9 +131,6 @@
                 anc_sems.at[2 * hop + 1],
                 dom=me ^ (t * stride),
             ).start()
-            return carry
-
-        lax.fori_loop(1, 8, start, 0)
 
     def anc_done(hop):
         view = anc_recv.at[hop, pl.ds(1, 7)]
@@ -125,23 +142,47 @@
 
     anc_hop(0, 8)
 
-    def spread(n, carry):
-        row = (n // 3) ^ my_row
-        i = lax.rem(n, 3)
-        target = holder_of(row, i, dp)
-        p = row * 3 + i
-
-        @pl.when(target != me)
-        def _():
-            remote(ens_ref.at[p], held.at[me], p1_send, p1_recv, dom=target).start()
-
-        @pl.when(target == me)
-        def _():
-            pltpu.make_async_copy(ens_ref.at[p], held.at[me], p1_send).start()
-
-        return carry
-
-    lax.fori_loop(0, TILES, spread, 0)
+    turn = 1 - 2 * (dp & 1)
+
+    def spread(z, rows):
+        def body(t, carry):
+            if z == 0:
+                y = (my_y + 8 + t * turn) & 7
+                row = y
+            else:
+                row = 8 + ((my_y + t) & 3)
+                y = (row + 7) & 7
+            for k in range(4):
+                x = my_x ^ k
+                p = row * 4 + x
+                target = join_dom(y, z, x)
+
+                @pl.when(target != me)
+                def _(p=p, target=target):
+                    remote(ens_ref.at[p], held.at[me], p1_send, p1_recv, dom=target).start()
+
+            return carry
+
+        lax.fori_loop(0, rows, body, 0)
+
+    @pl.when(my_z == 0)
+    def _():
+        spread(1, 4)
+        spread(0, 8)
+
+    @pl.when(my_z == 1)
+    def _():
+        spread(0, 8)
+        spread(1, 4)
+
+    own_plane = pltpu.make_async_copy(ens_ref.at[my_tile], held.at[me], local_sem.at[0])
+
+    @pl.when(is_holder)
+    def _():
+        own_plane.start()
+
+    anc_send[1] = anc_done(0)
+    anc_hop(1, 1)
 
     coefs = (dif_ref, spd_ref, per_ref)
 
@@ -163,9 +204,6 @@
             depth=dp + 1,
         )
 
-    anc_send[1] = anc_done(0)
-    anc_hop(1, 1)
-
     @pl.when(has_low)
     def _():
         for c in range(3):
@@ -177,37 +215,45 @@
             coef_to_high(c).start()
 
     anc_row[...] = anc_done(1)
-    to_smem = pltpu.make_async_copy(anc_row, anc_smem, smem_sem)
+    to_smem = pltpu.make_async_copy(anc_row, anc_all, smem_sem)
     to_smem.start()
     to_smem.wait()
 
-    state_tiles = state_ref
-
-    f = my_tile // 12
-    rest = lax.rem(my_tile, 12)
-    layer = rest // 2 + HALO
-    half = lax.rem(rest, 2)
-
-    pltpu.make_async_copy(held.at[pl.ds(0, TILES)], held.at[pl.ds(0, TILES)], p1_send).wait()
+    f = my_tile // (2 * LAYERS)
+    layer = HALO + lax.rem(my_tile, 2 * LAYERS) // 2
+    half = lax.rem(my_tile, 2)
 
     @pl.when(is_holder)
     def _():
-        pltpu.make_async_copy(
-            held.at[pl.ds(0, DOM - 1)], held.at[pl.ds(0, DOM - 1)], p1_recv
-        ).wait()
-        place = state_tiles.at[f, layer, half]
-
-        def give(t, carry):
-            target = me ^ t
-            out_tiles[t] = held[anc_smem[0, target]]
-            remote(out_tiles.at[t], place, p2_send, p2_recv, dom=target).start()
-            return carry
-
-        lax.fori_loop(1, DOM, give, 0)
-        out_tiles[0] = held[anc_smem[0, me]]
-        pltpu.make_async_copy(out_tiles.at[0], place, p2_recv).start()
-
-    own = held.at[pl.ds(0, TILES)]
+        others = held.at[pl.ds(0, DOM - 1)]
+        pltpu.make_async_copy(others, others, p1_recv).wait()
+        own_plane.wait()
+        place = state_ref.at[f, layer, half]
+
+        def give(z):
+            def body(t, carry):
+                y = (my_y + 8 + t * turn) & 7
+                for k in range(4):
+                    n = z * 32 + t * 4 + k
+                    target = join_dom(y, z, my_x ^ k)
+                    chosen[n] = held[anc_all[0, target]]
+
+                    @pl.when(target != me)
+                    def _(n=n, target=target):
+                        remote(chosen.at[n], place, p2_send, p2_recv, dom=target).start()
+
+                    @pl.when(target == me)
+                    def _(n=n):
+                        pltpu.make_async_copy(chosen.at[n], place, p2_recv).start()
+
+                return carry
+
+            lax.fori_loop(0, 8, body, 0)
+
+        give(0)
+        give(1)
+
+    own = held.at[pl.ds(0, HOLDERS)]
     pltpu.make_async_copy(own, own, p2_recv).wait()
 
     to_low = remote(
@@ -235,8 +281,15 @@
 
     @pl.when(is_holder)
     def _():
-        sent = out_tiles.at[pl.ds(1, DOM - 1)]
+        sent = held.at[pl.ds(0, HOLDERS - 1)]
+        pltpu.make_async_copy(sent, sent, p1_send).wait()
+        sent = chosen.at[pl.ds(0, DOM - 1)]
         pltpu.make_async_copy(sent, sent, p2_send).wait()
+
+    @pl.when(jnp.logical_not(is_holder))
+    def _():
+        sent = held.at[pl.ds(0, HOLDERS)]
+        pltpu.make_async_copy(sent, sent, p1_send).wait()
 
     for hop in range(2):
         view = anc_recv.at[hop, pl.ds(1, 7)]
@@ -329,7 +382,7 @@
 
 def local(ancestors, ensemble, diffusivity, melting_speed, permeability):
     any_spec = pl.BlockSpec(memory_space=pl.ANY)
-    tiles = ensemble.reshape(TILES, TILE, NY)
+    tiles = ensemble.reshape(HOLDERS, TILE, NY)
     split = (LAYERS, NX // TILE, TILE, NY)
     coefs = [c.reshape(split) for c in (diffusivity, melting_speed, permeability)]
     dma = pltpu.SemaphoreType.DMA
@@ -352,6 +405,7 @@
             dma,
             dma,
             dma,
+            dma((1,)),
             dma,
             dma,
             dma((2,)),

time: 49.2 us -> 45 us (0.915)
  Pallas kernels: 48.4 us -> 44.2 us
    pallas_call x1, Pallas kernels: 45.8 us -> 41.6 us  [local(): pl.pallas_call(resample_kernel, out_shape=(jax.ShapeDtypeStruct((FIELDS,...]
where the time goes in v2:
time: 45 us; the launch traced here: 44.8 us
  Pallas kernels  44.2 us (98%)
  between operations  0.66 us (1%)
    pallas_call x1, Pallas kernels, local(): pl.pallas_call(resample_kernel, out_shape=(jax.ShapeDtypeStruct((FIELDS,...  41.6 us
    pallas_call x1, Pallas kernels, local(): pl.pallas_call(forecast_kernel, out_shape=jax.ShapeDtypeStruct((FIELDS, L...  2.6 us

profile of v2, /device:TPU:1, one launch (start us, length us, event | category | flops | bytes accessed | tf_op | source)
XLA Modules:
  0.0 44.8 jit_solution(13229953586735182487)
XLA Ops:
  0.7 41.6 %shard_map.55 = (f32[4,14,2,8,128]{4,3,2,1,0:T(8,128)}, f32[2,3,3,2,8,128]{5,4,3,2,1,0:T(8,128)}) custom-call(s32[1]{0:T(128)S(6)} %copy.6.anc_ref, f32[48,8,128]{2,1,0:T(8,128)} %bitcast.8, f32[6,2,8,128]{3,2,1,0:T(8,128)} %bitcast.9, f32[6,2,8,128]{3,2,1,0:T(8,128)} %bitcast.10, f32[6,2,8,128]{3,2,1,0:T(8,128)} %bitcast.11), custom_call_target="tpu_custom_call" | custom-call | tf_op jit(solution)/shard_map/pallas_call | solution.py:389
  42.2 2.6 %shard_map.56 = f32[4,6,16,128]{3,2,1,0:T(8,128)} custom-call(f32[4,14,16,128]{3,2,1,0:T(8,128)} %bitcast.7, f32[2,3,3,16,128]{4,3,2,1,0:T(8,128)} %bitcast.12, f32[6,16,128]{2,1,0:T(8,128)} %dif_ref.1, f32[6,16,128]{2,1,0:T(8,128)} %spd_ref.1, f32[6,16,128]{2,1,0:T(8,128)} %per_ref.1), custom_call_target="tpu_custom_call" | custom-call | tf_op jit(solution)/shard_map/pallas_call | solution.py:421

commit v3 on v2

--- a/solution.py
+++ b/solution.py
@@ -50,6 +50,8 @@
     coef_ref,
     held,
     chosen,
+    mine,
+    mine_sem,
     anc_send,
     anc_recv,
     anc_row,
@@ -65,15 +67,28 @@
     halo_recv,
     coef_send,
     coef_recv,
+    own_coef_sem,
 ):
     me = lax.axis_index("dom")
     dp = lax.axis_index("depth")
     my_y, my_z, my_x = split_dom(me)
-    my_tile = jnp.where(my_z == 0, my_y, DOM // 8 + lax.rem(my_y + 1, 8)) * 4 + my_x
-    is_holder = my_tile < HOLDERS
+    near = (my_y + 2) & 7
+    late_holder = ((my_x != 2) & (near < 5)) | ((my_x == 2) & (my_y == 0))
+    late_tile = jnp.where(my_x == 2, HOLDERS - 1, DOM // 2 + near * 3 + my_x - my_x // 3)
+    my_tile = jnp.where(my_z == 0, my_y * 4 + my_x, late_tile)
+    is_holder = (my_z == 0) | late_holder
     has_low = dp > 0
     has_high = dp < DEPTH - 1
 
+    fetch = pltpu.make_async_copy(ens_ref, mine, mine_sem)
+    fetch.start()
+    coefs = (dif_ref, spd_ref, per_ref)
+    own_coefs = [
+        pltpu.make_async_copy(
+            coefs[c], coef_ref.at[c, pl.ds(COEF_HALO, LAYERS)], own_coef_sem.at[c]
+        )
+        for c in range(3)
+    ]
     barrier = pltpu.get_barrier_semaphore()
 
     def greet(t, carry):
@@ -87,7 +102,18 @@
 
     @pl.when(is_holder)
     def _():
-        lax.fori_loop(1, DOM, greet, 0)
+        def greet_row(t, carry):
+            for z in (1, 0):
+                for k in range(4):
+                    greet(t * 8 + z * 4 + k, 0)
+            return carry
+
+        for t in (4, 5, 3, 6, 2, 7, 1):
+            greet_row(t, 0)
+        for k in range(4):
+            greet(4 + k, 0)
+        for k in range(1, 4):
+            greet(k, 0)
 
     @pl.when(jnp.logical_not(is_holder))
     def _():
@@ -110,13 +136,14 @@
     lane = lax.broadcasted_iota(jnp.int32, (1, 128), 1)
     anc_send[0] = jnp.where(lane == me, anc_ref[0], 0)
     other = jnp.where(is_holder, 0, 1)
-    far_row = jnp.where((my_y >= 3) & (my_y <= 6), 1, 0)
+    column = my_z * jnp.where(my_x == 2, 7, 3)
+    row = jnp.where(my_y == 0, 0, jnp.where(near < 5, 1, 4))
     pl.semaphore_wait(
         barrier,
         HOLDERS
         - is_holder.astype(jnp.int32)
-        + 4 * my_z
-        + 4 * far_row
+        + column
+        + row
         - 2 * other
         + has_low.astype(jnp.int32)
         + has_high.astype(jnp.int32),
@@ -141,41 +168,45 @@
         return total
 
     anc_hop(0, 8)
+    fetch.wait()
 
     turn = 1 - 2 * (dp & 1)
 
-    def spread(z, rows):
+    def send_tile(p, target):
+        @pl.when(target != me)
+        def _():
+            remote(mine.at[p], held.at[me], p1_send, p1_recv, dom=target).start()
+
+    def spread_early():
         def body(t, carry):
-            if z == 0:
-                y = (my_y + 8 + t * turn) & 7
-                row = y
-            else:
-                row = 8 + ((my_y + t) & 3)
-                y = (row + 7) & 7
+            y = (my_y + 12 + t * turn) & 7
             for k in range(4):
                 x = my_x ^ k
-                p = row * 4 + x
-                target = join_dom(y, z, x)
-
-                @pl.when(target != me)
-                def _(p=p, target=target):
-                    remote(ens_ref.at[p], held.at[me], p1_send, p1_recv, dom=target).start()
-
+                send_tile(y * 4 + x, join_dom(y, 0, x))
             return carry
 
-        lax.fori_loop(0, rows, body, 0)
+        lax.fori_loop(0, 8, body, 0)
+
+    def spread_late():
+        def body(t, carry):
+            for i in range(3):
+                send_tile(DOM // 2 + t * 3 + i, join_dom((t + 6) & 7, 1, i + i // 2))
+            return carry
+
+        lax.fori_loop(0, 5, body, 0)
+        send_tile(HOLDERS - 1, join_dom(0, 1, 2))
 
     @pl.when(my_z == 0)
     def _():
-        spread(1, 4)
-        spread(0, 8)
+        spread_late()
+        spread_early()
 
     @pl.when(my_z == 1)
     def _():
-        spread(0, 8)
-        spread(1, 4)
-
-    own_plane = pltpu.make_async_copy(ens_ref.at[my_tile], held.at[me], local_sem.at[0])
+        spread_early()
+        spread_late()
+
+    own_plane = pltpu.make_async_copy(mine.at[my_tile], held.at[me], local_sem.at[0])
 
     @pl.when(is_holder)
     def _():
@@ -183,13 +214,14 @@
 
     anc_send[1] = anc_done(0)
     anc_hop(1, 1)
-
-    coefs = (dif_ref, spd_ref, per_ref)
+    for copy in own_coefs:
+        copy.start()
+
 
     def coef_to_low(c):
         return remote(
             coefs[c].at[pl.ds(0, COEF_HALO)],
-            coef_ref.at[1, c],
+            coef_ref.at[c, pl.ds(COEF_HALO + LAYERS, COEF_HALO)],
             coef_send.at[0, c],
             coef_recv.at[1, c],
             depth=dp - 1,
@@ -198,7 +230,7 @@
     def coef_to_high(c):
         return remote(
             coefs[c].at[pl.ds(LAYERS - COEF_HALO, COEF_HALO)],
-            coef_ref.at[0, c],
+            coef_ref.at[c, pl.ds(0, COEF_HALO)],
             coef_send.at[1, c],
             coef_recv.at[0, c],
             depth=dp + 1,
@@ -240,11 +272,11 @@
 
                     @pl.when(target != me)
                     def _(n=n, target=target):
-                        remote(chosen.at[n], place, p2_send, p2_recv, dom=target).start()
+                        remote(chosen.at[n], place, p2_send, p2_recv.at[f], dom=target).start()
 
                     @pl.when(target == me)
                     def _(n=n):
-                        pltpu.make_async_copy(chosen.at[n], place, p2_recv).start()
+                        pltpu.make_async_copy(chosen.at[n], place, p2_recv.at[f]).start()
 
                 return carry
 
@@ -253,31 +285,35 @@
         give(0)
         give(1)
 
-    own = held.at[pl.ds(0, HOLDERS)]
-    pltpu.make_async_copy(own, own, p2_recv).wait()
-
-    to_low = remote(
-        state_ref.at[:, pl.ds(HALO, HALO)],
-        state_ref.at[:, pl.ds(HALO + LAYERS, HALO)],
-        halo_send.at[0],
-        halo_recv.at[1],
-        depth=dp - 1,
-    )
-    to_high = remote(
-        state_ref.at[:, pl.ds(LAYERS, HALO)],
-        state_ref.at[:, pl.ds(0, HALO)],
-        halo_send.at[1],
-        halo_recv.at[0],
-        depth=dp + 1,
-    )
-
-    @pl.when(has_low)
-    def _():
-        to_low.start()
-
-    @pl.when(has_high)
-    def _():
-        to_high.start()
+    def to_low(field):
+        return remote(
+            state_ref.at[field, pl.ds(HALO, HALO)],
+            state_ref.at[field, pl.ds(HALO + LAYERS, HALO)],
+            halo_send.at[0, field],
+            halo_recv.at[1, field],
+            depth=dp - 1,
+        )
+
+    def to_high(field):
+        return remote(
+            state_ref.at[field, pl.ds(LAYERS, HALO)],
+            state_ref.at[field, pl.ds(0, HALO)],
+            halo_send.at[1, field],
+            halo_recv.at[0, field],
+            depth=dp + 1,
+        )
+
+    for field in range(FIELDS):
+        own = held.at[pl.ds(0, HOLDERS // FIELDS)]
+        pltpu.make_async_copy(own, own, p2_recv.at[field]).wait()
+
+        @pl.when(has_low)
+        def _(field=field):
+            to_low(field).start()
+
+        @pl.when(has_high)
+        def _(field=field):
+            to_high(field).start()
 
     @pl.when(is_holder)
     def _():
@@ -291,6 +327,9 @@
         sent = held.at[pl.ds(0, HOLDERS)]
         pltpu.make_async_copy(sent, sent, p1_send).wait()
 
+    for copy in own_coefs:
+        copy.wait()
+
     for hop in range(2):
         view = anc_recv.at[hop, pl.ds(1, 7)]
         pltpu.make_async_copy(view, view, anc_sems.at[2 * hop]).wait()
@@ -300,19 +339,21 @@
         for c in range(3):
             coef_to_low(c).wait_send()
             coef_to_high(c).wait_recv()
-        to_low.wait_send()
-        to_high.wait_recv()
+        for field in range(FIELDS):
+            to_low(field).wait_send()
+            to_high(field).wait_recv()
 
     @pl.when(has_high)
     def _():
         for c in range(3):
             coef_to_high(c).wait_send()
             coef_to_low(c).wait_recv()
-        to_high.wait_send()
-        to_low.wait_recv()
-
-
-def forecast_kernel(state_ref, halo_ref, dif_ref, spd_ref, per_ref, out_ref, a_ref, b_ref):
+        for field in range(FIELDS):
+            to_high(field).wait_send()
+            to_low(field).wait_recv()
+
+
+def forecast_kernel(state_ref, coef_ref, out_ref, a_ref, b_ref):
     dp = lax.axis_index("depth")
     has_low = dp > 0
     has_high = dp < DEPTH - 1
@@ -320,14 +361,9 @@
     col = lax.broadcasted_iota(jnp.int32, (NX, NY), 1)
     first_row, last_row = row == 0, row == NX - 1
     first_col, last_col = col == 0, col == NY - 1
-    inner = (dif_ref, spd_ref, per_ref)
 
     def coef(c, e):
-        if e < HALO:
-            return halo_ref[0, c, e - (HALO - COEF_HALO)]
-        if e >= HALO + LAYERS:
-            return halo_ref[1, c, e - HALO - LAYERS]
-        return inner[c][e - HALO]
+        return coef_ref[c, e - (HALO - COEF_HALO)]
 
     def inside(e, x):
         if e < HALO:
@@ -386,17 +422,19 @@
     split = (LAYERS, NX // TILE, TILE, NY)
     coefs = [c.reshape(split) for c in (diffusivity, melting_speed, permeability)]
     dma = pltpu.SemaphoreType.DMA
-    state, halo = pl.pallas_call(
+    state, coefs = pl.pallas_call(
         resample_kernel,
         out_shape=(
-            jax.ShapeDtypeStruct((FIELDS, EXT, NX // TILE, TILE, NY), jnp.float32),
-            jax.ShapeDtypeStruct((2, 3, COEF_HALO, NX // TILE, TILE, NY), jnp.float32),
+            pltpu.VMEM((FIELDS, EXT, NX // TILE, TILE, NY), jnp.float32),
+            pltpu.VMEM((3, LAYERS + 2 * COEF_HALO, NX // TILE, TILE, NY), jnp.float32),
         ),
         in_specs=[pl.BlockSpec(memory_space=pltpu.SMEM)] + [any_spec] * 4,
-        out_specs=(any_spec, any_spec),
+        out_specs=(pl.BlockSpec(memory_space=pltpu.VMEM),) * 2,
         scratch_shapes=[
             pltpu.VMEM((DOM, TILE, NY), jnp.float32),
             pltpu.VMEM((DOM, TILE, NY), jnp.float32),
+            pltpu.VMEM((HOLDERS, TILE, NY), jnp.float32),
+            dma,
             pltpu.VMEM((2, 1, 128), jnp.int32),
             pltpu.VMEM((2, 8, 1, 128), jnp.int32),
             pltpu.VMEM((1, 128), jnp.int32),
@@ -407,24 +445,26 @@
             dma,
             dma((1,)),
             dma,
-            dma,
-            dma((2,)),
-            dma((2,)),
+            dma((FIELDS,)),
+            dma((2, FIELDS)),
+            dma((2, FIELDS)),
             dma((2, 3)),
             dma((2, 3)),
+            dma((3,)),
         ],
         compiler_params=pltpu.CompilerParams(collective_id=0, has_side_effects=True),
     )(ancestors, tiles, *coefs)
     state = state.reshape(FIELDS, EXT, NX, NY)
-    halo = halo.reshape(2, 3, COEF_HALO, NX, NY)
+    coefs = coefs.reshape(3, LAYERS + 2 * COEF_HALO, NX, NY)
     vmem = pl.BlockSpec(memory_space=pltpu.VMEM)
+    pin, space = pltpu.with_memory_space_constraint, pltpu.VMEM
     out = pl.pallas_call(
         forecast_kernel,
         out_shape=jax.ShapeDtypeStruct((FIELDS, LAYERS, NX, NY), jnp.float32),
-        in_specs=[vmem] * 5,
+        in_specs=[vmem] * 2,
         out_specs=vmem,
         scratch_shapes=[pltpu.VMEM((FIELDS, EXT, NX, NY), jnp.float32)] * 2,
-    )(state, halo, diffusivity, melting_speed, permeability)
+    )(pin(state, space), pin(coefs, space))
     return out[None]
 
 

time: 45 us -> 42.3 us (0.940)
  Pallas kernels: 44.2 us -> 41.5 us
    pallas_call x1, Pallas kernels: 41.6 us -> 40 us  [local(): pl.pallas_call(resample_kernel, out_shape=(pltpu.VMEM((FIELDS, EXT, NX //...]
    pallas_call x1, Pallas kernels: 2.6 us -> 1.47 us  [local(): pl.pallas_call(forecast_kernel, out_shape=jax.ShapeDtypeStruct((FIELDS, L...]
where the time goes in v3:
time: 42.3 us; the launch traced here: 42.2 us
  Pallas kernels  41.5 us (98%)
  between operations  0.66 us (2%)
    pallas_call x1, Pallas kernels, local(): pl.pallas_call(resample_kernel, out_shape=(pltpu.VMEM((FIELDS, EXT, NX //...  40 us
    pallas_call x1, Pallas kernels, local(): pl.pallas_call(forecast_kernel, out_shape=jax.ShapeDtypeStruct((FIELDS, L...  1.47 us

profile of v3, /device:TPU:1, one launch (start us, length us, event | category | flops | bytes accessed | tf_op | source)
XLA Modules:
  0.0 42.2 jit_solution(5438142812913279917)
XLA Ops:
  0.7 40.0 %shard_map.55 = (f32[4,14,2,8,128]{4,3,2,1,0:T(8,128)S(1)}, f32[3,12,2,8,128]{4,3,2,1,0:T(8,128)S(1)}) custom-call(s32[1]{0:T(128)S(6)} %copy.6.anc_ref, f32[48,8,128]{2,1,0:T(8,128)} %bitcast.9, f32[6,2,8,128]{3,2,1,0:T(8,128)} %bitcast.10, f32[6,2,8,128]{3,2,1,0:T(8,128)} %bitcast.11, f32[6,2,8,128]{3,2,1,0:T(8,128)} %bitcast.12), custom_call_target="tpu_custom_call" | custom-call | tf_op jit(solution)/shard_map/pallas_call | solution.py:425
  40.7 1.5 %shard_map.56 = f32[4,6,16,128]{3,2,1,0:T(8,128)} custom-call(f32[4,14,16,128]{3,2,1,0:T(8,128)S(1)} %bitcast.7, f32[3,12,16,128]{3,2,1,0:T(8,128)S(1)} %bitcast.8), custom_call_target="tpu_custom_call" | custom-call | tf_op jit(solution)/shard_map/pallas_call | solution.py:461

commit v4 on v3

--- a/solution.py
+++ b/solution.py
@@ -68,6 +68,7 @@
     coef_send,
     coef_recv,
     own_coef_sem,
+    cross,
 ):
     me = lax.axis_index("dom")
     dp = lax.axis_index("depth")
@@ -100,26 +101,19 @@
         )
         return carry
 
-    @pl.when(is_holder)
-    def _():
-        def greet_row(t, carry):
-            for z in (1, 0):
-                for k in range(4):
-                    greet(t * 8 + z * 4 + k, 0)
+    for t in (4, 5, 3, 6, 2, 7, 1):
+        greet(8 * t, 0)
+    for t in (2, 3, 1):
+        greet(t, 0)
+
+    @pl.when(my_z == 0)
+    def _():
+        def greet_late(t, carry):
+            for k in range(4):
+                greet(t * 8 + 4 + k, 0)
             return carry
 
-        for t in (4, 5, 3, 6, 2, 7, 1):
-            greet_row(t, 0)
-        for k in range(4):
-            greet(4 + k, 0)
-        for k in range(1, 4):
-            greet(k, 0)
-
-    @pl.when(jnp.logical_not(is_holder))
-    def _():
-        for t in range(1, 8):
-            greet(t, 0)
-            greet(8 * t, 0)
+        lax.fori_loop(0, 8, greet_late, 0)
 
     @pl.when(has_low)
     def _():
@@ -135,16 +129,10 @@
 
     lane = lax.broadcasted_iota(jnp.int32, (1, 128), 1)
     anc_send[0] = jnp.where(lane == me, anc_ref[0], 0)
-    other = jnp.where(is_holder, 0, 1)
-    column = my_z * jnp.where(my_x == 2, 7, 3)
-    row = jnp.where(my_y == 0, 0, jnp.where(near < 5, 1, 4))
     pl.semaphore_wait(
         barrier,
-        HOLDERS
-        - is_holder.astype(jnp.int32)
-        + column
-        + row
-        - 2 * other
+        10
+        + DOM // 2 * my_z
         + has_low.astype(jnp.int32)
         + has_high.astype(jnp.int32),
     )
@@ -168,7 +156,6 @@
         return total
 
     anc_hop(0, 8)
-    fetch.wait()
 
     turn = 1 - 2 * (dp & 1)
 
@@ -196,15 +183,28 @@
         lax.fori_loop(0, 5, body, 0)
         send_tile(HOLDERS - 1, join_dom(0, 1, 2))
 
+    fetch.wait()
+
+    @pl.when(my_z == 1)
+    def _():
+        for k in range(4):
+            pl.semaphore_signal(
+                cross,
+                inc=1,
+                device_id={"dom": me ^ (4 + k)},
+                device_id_type=pl.DeviceIdType.MESH,
+            )
+        spread_early()
+
+    anc_send[1] = anc_done(0)
+
     @pl.when(my_z == 0)
     def _():
-        spread_late()
         spread_early()
-
-    @pl.when(my_z == 1)
-    def _():
-        spread_early()
-        spread_late()
+        pl.semaphore_wait(cross, 4)
+
+    anc_hop(1, 1)
+    spread_late()
 
     own_plane = pltpu.make_async_copy(mine.at[my_tile], held.at[me], local_sem.at[0])
 
@@ -212,8 +212,6 @@
     def _():
         own_plane.start()
 
-    anc_send[1] = anc_done(0)
-    anc_hop(1, 1)
     for copy in own_coefs:
         copy.start()
 
@@ -451,6 +449,7 @@
             dma((2, 3)),
             dma((2, 3)),
             dma((3,)),
+            pltpu.SemaphoreType.REGULAR,
         ],
         compiler_params=pltpu.CompilerParams(collective_id=0, has_side_effects=True),
     )(ancestors, tiles, *coefs)

time: 42.3 us -> 41.2 us (0.974)
  Pallas kernels: 41.5 us -> 40.4 us
    pallas_call x1, Pallas kernels: 40 us -> 39 us  [local(): pl.pallas_call(resample_kernel, out_shape=(pltpu.VMEM((FIELDS, EXT, NX //...]
where the time goes in v4:
time: 41.2 us; the launch traced here: 41.1 us
  Pallas kernels  40.4 us (98%)
  between operations  0.66 us (2%)
    pallas_call x1, Pallas kernels, local(): pl.pallas_call(resample_kernel, out_shape=(pltpu.VMEM((FIELDS, EXT, NX //...  39 us
    pallas_call x1, Pallas kernels, local(): pl.pallas_call(forecast_kernel, out_shape=jax.ShapeDtypeStruct((FIELDS, L...  1.47 us

profile of v4, /device:TPU:1, one launch (start us, length us, event | category | flops | bytes accessed | tf_op | source)
XLA Modules:
  0.0 41.1 jit_solution(2480392232565285130)
XLA Ops:
  0.7 39.0 %shard_map.55 = (f32[4,14,2,8,128]{4,3,2,1,0:T(8,128)S(1)}, f32[3,12,2,8,128]{4,3,2,1,0:T(8,128)S(1)}) custom-call(s32[1]{0:T(128)S(6)} %copy.6.anc_ref, f32[48,8,128]{2,1,0:T(8,128)} %bitcast.9, f32[6,2,8,128]{3,2,1,0:T(8,128)} %bitcast.10, f32[6,2,8,128]{3,2,1,0:T(8,128)} %bitcast.11, f32[6,2,8,128]{3,2,1,0:T(8,128)} %bitcast.12), custom_call_target="tpu_custom_call" | custom-call | tf_op jit(solution)/shard_map/pallas_call | solution.py:423
  39.6 1.5 %shard_map.56 = f32[4,6,16,128]{3,2,1,0:T(8,128)} custom-call(f32[4,14,16,128]{3,2,1,0:T(8,128)S(1)} %bitcast.7, f32[3,12,16,128]{3,2,1,0:T(8,128)S(1)} %bitcast.8), custom_call_target="tpu_custom_call" | custom-call | tf_op jit(solution)/shard_map/pallas_call | solution.py:460

commit v5 on v4

--- a/solution.py
+++ b/solution.py
@@ -157,6 +157,43 @@
 
     anc_hop(0, 8)
 
+
+    def coef_to_low(c):
+        return remote(
+            coefs[c].at[pl.ds(0, COEF_HALO)],
+            coef_ref.at[c, pl.ds(COEF_HALO + LAYERS, COEF_HALO)],
+            coef_send.at[0, c],
+            coef_recv.at[1, c],
+            depth=dp - 1,
+        )
+
+    def coef_to_high(c):
+        return remote(
+            coefs[c].at[pl.ds(LAYERS - COEF_HALO, COEF_HALO)],
+            coef_ref.at[c, pl.ds(0, COEF_HALO)],
+            coef_send.at[1, c],
+            coef_recv.at[0, c],
+            depth=dp + 1,
+        )
+
+    def start_coefs():
+        for copy in own_coefs:
+            copy.start()
+
+        @pl.when(has_low)
+        def _():
+            for c in range(3):
+                coef_to_low(c).start()
+
+        @pl.when(has_high)
+        def _():
+            for c in range(3):
+                coef_to_high(c).start()
+
+    @pl.when(my_z == 0)
+    def _():
+        start_coefs()
+
     turn = 1 - 2 * (dp & 1)
 
     def send_tile(p, target):
@@ -212,37 +249,10 @@
     def _():
         own_plane.start()
 
-    for copy in own_coefs:
-        copy.start()
-
-
-    def coef_to_low(c):
-        return remote(
-            coefs[c].at[pl.ds(0, COEF_HALO)],
-            coef_ref.at[c, pl.ds(COEF_HALO + LAYERS, COEF_HALO)],
-            coef_send.at[0, c],
-            coef_recv.at[1, c],
-            depth=dp - 1,
-        )
-
-    def coef_to_high(c):
-        return remote(
-            coefs[c].at[pl.ds(LAYERS - COEF_HALO, COEF_HALO)],
-            coef_ref.at[c, pl.ds(0, COEF_HALO)],
-            coef_send.at[1, c],
-            coef_recv.at[0, c],
-            depth=dp + 1,
-        )
-
-    @pl.when(has_low)
-    def _():
-        for c in range(3):
-            coef_to_low(c).start()
-
-    @pl.when(has_high)
-    def _():
-        for c in range(3):
-            coef_to_high(c).start()
+
+    @pl.when(my_z == 1)
+    def _():
+        start_coefs()
 
     anc_row[...] = anc_done(1)
     to_smem = pltpu.make_async_copy(anc_row, anc_all, smem_sem)
@@ -260,28 +270,34 @@
         own_plane.wait()
         place = state_ref.at[f, layer, half]
 
-        def give(z):
+        def send(n, target):
+            chosen[n] = held[anc_all[0, target]]
+            remote(chosen.at[n], place, p2_send, p2_recv.at[f], dom=target).start()
+
+        def give(z, mine_first):
             def body(t, carry):
                 y = (my_y + 8 + t * turn) & 7
                 for k in range(4):
-                    n = z * 32 + t * 4 + k
-                    target = join_dom(y, z, my_x ^ k)
-                    chosen[n] = held[anc_all[0, target]]
-
-                    @pl.when(target != me)
-                    def _(n=n, target=target):
-                        remote(chosen.at[n], place, p2_send, p2_recv.at[f], dom=target).start()
-
-                    @pl.when(target == me)
-                    def _(n=n):
-                        pltpu.make_async_copy(chosen.at[n], place, p2_recv.at[f]).start()
-
+                    send(z * 32 + t * 4 + k, join_dom(y, z, my_x ^ k))
                 return carry
 
-            lax.fori_loop(0, 8, body, 0)
-
-        give(0)
-        give(1)
+            if mine_first:
+                n = z * 32
+                chosen[n] = held[anc_all[0, me]]
+                pltpu.make_async_copy(chosen.at[n], place, p2_recv.at[f]).start()
+                for k in range(1, 4):
+                    send(n + k, join_dom(my_y, z, my_x ^ k))
+            lax.fori_loop(1 if mine_first else 0, 8, body, 0)
+
+        @pl.when(my_z == 0)
+        def _():
+            give(0, True)
+            give(1, False)
+
+        @pl.when(my_z == 1)
+        def _():
+            give(0, False)
+            give(1, True)
 
     def to_low(field):
         return remote(

time: 41.2 us -> 41 us (level)
  no operation moved by 1% of the time
where the time goes in v5:
time: 41 us; the launch traced here: 40.9 us
  Pallas kernels  40.2 us (98%)
  between operations  0.66 us (2%)
    pallas_call x1, Pallas kernels, local(): pl.pallas_call(resample_kernel, out_shape=(pltpu.VMEM((FIELDS, EXT, NX //...  38.8 us
    pallas_call x1, Pallas kernels, local(): pl.pallas_call(forecast_kernel, out_shape=jax.ShapeDtypeStruct((FIELDS, L...  1.47 us

profile of v5, /device:TPU:1, one launch (start us, length us, event | category | flops | bytes accessed | tf_op | source)
XLA Modules:
  0.0 40.9 jit_solution(8032307620466627146)
XLA Ops:
  0.7 38.8 %shard_map.55 = (f32[4,14,2,8,128]{4,3,2,1,0:T(8,128)S(1)}, f32[3,12,2,8,128]{4,3,2,1,0:T(8,128)S(1)}) custom-call(s32[1]{0:T(128)S(6)} %copy.6.anc_ref, f32[48,8,128]{2,1,0:T(8,128)} %bitcast.9, f32[6,2,8,128]{3,2,1,0:T(8,128)} %bitcast.10, f32[6,2,8,128]{3,2,1,0:T(8,128)} %bitcast.11, f32[6,2,8,128]{3,2,1,0:T(8,128)} %bitcast.12), custom_call_target="tpu_custom_call" | custom-call | tf_op jit(solution)/shard_map/pallas_call | solution.py:439
  39.4 1.5 %shard_map.56 = f32[4,6,16,128]{3,2,1,0:T(8,128)} custom-call(f32[4,14,16,128]{3,2,1,0:T(8,128)S(1)} %bitcast.7, f32[3,12,16,128]{3,2,1,0:T(8,128)S(1)} %bitcast.8), custom_call_target="tpu_custom_call" | custom-call | tf_op jit(solution)/shard_map/pallas_call | solution.py:476
